TPU v7x, 512 devices: a whole 4x8x8 slice. The times are simulated.
512 devices in a mesh: dev: 32 (over y_hi, z), ha: 2 (over y_lo), col: 8 (over x, core).
Axes of the slice: x: 4, y: 8 (y_hi: 4, y_lo: 2; y = y_hi * 2 + y_lo), z: 8, core: 2. Of those that a mesh axis runs over, the one named last changes fastest.
Arguments:
- features: bfloat16 [128, 128, 32, 128], P('col', 'dev', 'ha'), may hold values from -6 to 6
- kernel: bfloat16 [3, 3, 3, 128, 128], P(None, None, None, 'col'), may hold values from -0.109375 to 0.109375
- channel_bias: float32 [128], P('col'), may hold values from -3 to 3
Outputs:
- activated: bfloat16 [128, 128, 32, 128], P('col', 'dev', 'ha')
All inputs are finite; a program needn't handle non-finite values.
Results may differ from a plain program's by a relative error of at most 0.005.
Values may be sent and summed in bfloat16 or wider, within the bound.
A program may use at most 64 MiB of HBM per device.

v0:
```python
import jax
import jax.numpy as jnp
from jax import lax
from jax.sharding import PartitionSpec as P


def with_halo(x, sides, width):
    for axis, dim in sides:
        devices, length = (lax.axis_size(axis), x.shape[dim])
        up = [(i, (i + 1) % devices) for i in range(devices - 1)]
        down = [(j, i) for i, j in up]
        last = lax.slice_in_dim(x, length - width, length, axis=dim)
        first = lax.slice_in_dim(x, 0, width, axis=dim)
        before = lax.ppermute(last, axis, up)
        after = lax.ppermute(first, axis, down)
        x = jnp.concatenate([before, x, after], axis=dim)
    return x


def convolve(padded, weights):
    depth_pad = padded.shape[1]
    height_pad = padded.shape[2]
    width_cells = padded.shape[3]
    outer = weights.shape[3]
    depth_cells = depth_pad - 2
    height_cells = height_pad - 2
    partial_sums = [
        jnp.zeros((outer, depth_cells, height_cells, width_cells), jnp.float32)
        for col_tap in range(3)
    ]
    for depth_tap in range(3):
        planes = padded[:, depth_tap : depth_tap + depth_cells]
        tap_out = lax.dot_general(
            weights[depth_tap], planes, (((3,), (0,)), ((), ())), preferred_element_type=jnp.float32
        )
        for row_tap in range(3):
            for col_tap in range(3):
                partial_sums[col_tap] = (
                    partial_sums[col_tap]
                    + tap_out[row_tap, col_tap, :, :, row_tap : row_tap + height_cells, :]
                )
    zero_column = jnp.zeros((outer, depth_cells, height_cells, 1), jnp.float32)
    from_left = jnp.concatenate([zero_column, partial_sums[0][..., :-1]], axis=3)
    from_right = jnp.concatenate([partial_sums[2][..., 1:], zero_column], axis=3)
    return partial_sums[1] + from_left + from_right


def finish(summed, offsets):
    summed = summed + offsets[:, None, None, None]
    return jnp.where(summed >= 0, summed, 0.3 * summed).astype(jnp.bfloat16)


def per_device(features, kernel, channel_bias):
    padded = with_halo(features, (("dev", 1), ("ha", 2)), 1)
    gathered = lax.all_gather(padded, "col", axis=0, tiled=True)
    return finish(convolve(gathered, kernel), channel_bias)


def solution(mesh):
    in_specs = (P("col", "dev", "ha", None), P(None, None, None, "col", None), P("col"))
    out_specs = P("col", "dev", "ha", None)
    return jax.shard_map(
        per_device, mesh=mesh, in_specs=in_specs, out_specs=out_specs, check_vma=False
    )
```

profile of v0, /device:TPU:1, one launch (start us, length us, event | category | flops | bytes accessed | tf_op | source)
XLA Modules:
  0.0 85.2 jit_solution(9481461446292273636)
XLA Ops:
  6.5 0.0 all-gather.2.cloned.1.call-start
  6.5 0.9 %fusion.24 = (bf16[16,1,16,128]{3,2,1,0:T(8,128)(2,1)S(1)}, bf16[16,1,16,128]{3,2,1,0:T(8,128)(2,1)S(1)}) fusion(bf16[16,4,16,128]{3,2,1,0:T(8,128)(2,1)} %param.3), kind=kLoop, calls=%fused_computation.61 | loop fusion | bytes 262144 | tf_op jit(solution)/shard_map/slice | solution.py:13
  7.5 4.8 %collective-permute-start = (bf16[16,1,16,128]{3,0,2,1:T(8,128)(2,1)S(1)}, bf16[16,1,16,128]{3,0,2,1:T(8,128)(2,1)S(1)}, u32[]{:S(2)}, u32[]{:S(2)}) collective-permute-start(bf16[16,1,16,128]{3,0,2,1:T(8,128)(2,1)S(1)} %copy.37), channel_id=1, source_target_pairs={{0,16},{16,32},{32,48},{48,64},{64,80},{80,96},{96,112},{112,128},... | collective-permute-start | bytes 196616 | tf_op jit(solution)/shard_map/ppermute | solution.py:14
  12.3 1.3 %collective-permute-start.1 = (bf16[16,1,16,128]{3,0,2,1:T(8,128)(2,1)S(1)}, bf16[16,1,16,128]{3,0,2,1:T(8,128)(2,1)S(1)}, u32[]{:S(2)}, u32[]{:S(2)}) collective-permute-start(bf16[16,1,16,128]{3,0,2,1:T(8,128)(2,1)S(1)} %copy.38), channel_id=1, source_target_pairs={{16,0},{32,16},{48,32},{64,48},{80,64},{96,80},{112,96},{128,112},... | collective-permute-start | bytes 196616 | tf_op jit(solution)/shard_map/ppermute | solution.py:15
  13.6 0.0 collective-permute-done
  13.6 1.1 %constant_dynamic-update-slice_fusion.1 = bf16[16,6,16,128]{3,0,2,1:T(8,128)(2,1)S(1)} fusion(bf16[16,6,16,128]{3,0,2,1:T(8,128)(2,1)S(1)} %constant_dynamic-update-slice_fusion.2, bf16[16,4,16,128]{3,2,1,0:T(8,128)(2,1)} %param.3), kind=kLoop, calls=%fused_computation.58 | loop fusion | bytes 524288
  14.8 3.2 %collective-permute-done.1 = bf16[16,1,16,128]{3,0,2,1:T(8,128)(2,1)S(1)} collective-permute-done((bf16[16,1,16,128]{3,0,2,1:T(8,128)(2,1)S(1)}, bf16[16,1,16,128]{3,0,2,1:T(8,128)(2,1)S(1)}, u32[]{:S(2)}, u32[]{:S(2)}) %collective-permute-start.1) | collective-permute-done | bytes 65568 | tf_op jit(solution)/shard_map/ppermute | solution.py:15
  18.0 3.2 %collective-permute-start.2 = (bf16[16,6,1,128]{3,0,2,1:T(8,128)(2,1)S(1)}, bf16[16,6,1,128]{3,0,2,1:T(8,128)(2,1)S(1)}, u32[]{:S(2)}, u32[]{:S(2)}) collective-permute-start(bf16[16,6,1,128]{3,0,2,1:T(8,128)(2,1)S(1)} %get-tuple-element.5), channel_id=1, source_target_pairs={{0,8},{1,9},{2,10},{3,11},{4,12},{5,13},{6,14},{7,15},{16,24},{17,... | collective-permute-start | bytes 73736 | tf_op jit(solution)/shard_map/ppermute | solution.py:14
  21.2 1.3 %collective-permute-start.3 = (bf16[16,6,1,128]{3,0,2,1:T(8,128)(2,1)S(1)}, bf16[16,6,1,128]{3,0,2,1:T(8,128)(2,1)S(1)}, u32[]{:S(2)}, u32[]{:S(2)}) collective-permute-start(bf16[16,6,1,128]{3,0,2,1:T(8,128)(2,1)S(1)} %get-tuple-element.6), channel_id=1, source_target_pairs={{8,0},{9,1},{10,2},{11,3},{12,4},{13,5},{14,6},{15,7},{24,16},{25,... | collective-permute-start | bytes 73736 | tf_op jit(solution)/shard_map/ppermute | solution.py:15
  22.5 0.0 collective-permute-done.2
  22.5 3.3 %collective-permute-done.3 = bf16[16,6,1,128]{3,0,2,1:T(8,128)(2,1)S(1)} collective-permute-done((bf16[16,6,1,128]{3,0,2,1:T(8,128)(2,1)S(1)}, bf16[16,6,1,128]{3,0,2,1:T(8,128)(2,1)S(1)}, u32[]{:S(2)}, u32[]{:S(2)}) %collective-permute-start.3) | collective-permute-done | bytes 24608 | tf_op jit(solution)/shard_map/ppermute | solution.py:15
  25.8 0.8 pad_maximum_fusion
  26.6 0.0 all-gather.2.cloned.1.call-update
  26.7 0.0 copy-start.1
  26.7 45.2 %all-gather.2.cloned.1.call-done = bf16[128,6,18,128]{3,0,2,1:T(8,128)(2,1)} async-done(((bf16[16,6,18,128]{3,0,2,1:T(8,128)(2,1)}), bf16[128,6,18,128]{3,0,2,1:T(8,128)(2,1)}) %all-gather.2.cloned.1.call-update) | async-done | bytes 3538960 | tf_op jit(solution)/shard_map/all_gather | solution.py:55
  71.9 0.0 copy-start
  71.9 2.7 %convolution_bitcast_fusion = f32[3,3,16,4,18,128]{5,2,4,3,1,0:T(8,128)S(1)} fusion(bf16[128,6,18,128]{3,0,2,1:T(8,128)(2,1)} %all-gather.2.cloned.1.call-done, bf16[3,3,3,16,128]{4,3,2,1,0:T(8,128)(2,1)} %param.4), kind=kOutput, calls=%fused_computation | convolution fusion | flops 339738624 | bytes 7704576 | tf_op jit(solution)/shard_map/dot_general | solution.py:33
  74.6 0.0 copy-done.1
  74.6 0.1 copy-done
  74.6 0.8 convolution_bitcast_fusion.1
  75.5 0.8 convolution_bitcast_fusion.2
  76.3 0.0 copy-start.2
  76.3 0.3 fusion.2
  76.7 0.3 fusion.8
  77.0 0.2 slice.191
  77.2 0.0 copy-done.2
  77.2 0.4 fusion
  77.6 0.8 copy.21
  (5 shorter events, 0.1 us)
Async XLA Ops:
  6.5 65.4 %all-gather.2.cloned.1.call-start = ((), (), s32[]{:S(2)}) async-start(), calls=%async_computation | async-start | bytes 3981312 | tf_op jit(solution)/shard_map/all_gather | solution.py:55
  7.5 6.2 %collective-permute-start = (bf16[16,1,16,128]{3,0,2,1:T(8,128)(2,1)S(1)}, bf16[16,1,16,128]{3,0,2,1:T(8,128)(2,1)S(1)}, u32[]{:S(2)}, u32[]{:S(2)}) collective-permute-start(bf16[16,1,16,128]{3,0,2,1:T(8,128)(2,1)S(1)} %copy.37), channel_id=1, source_target_pairs={{0,16},{16,32},{32,48},{48,64},{64,80},{80,96},{96,112},{112,128},... | collective-permute-start | bytes 196616 | tf_op jit(solution)/shard_map/ppermute | solution.py:14
  12.3 5.6 %collective-permute-start.1 = (bf16[16,1,16,128]{3,0,2,1:T(8,128)(2,1)S(1)}, bf16[16,1,16,128]{3,0,2,1:T(8,128)(2,1)S(1)}, u32[]{:S(2)}, u32[]{:S(2)}) collective-permute-start(bf16[16,1,16,128]{3,0,2,1:T(8,128)(2,1)S(1)} %copy.38), channel_id=1, source_target_pairs={{16,0},{32,16},{48,32},{64,48},{80,64},{96,80},{112,96},{128,112},... | collective-permute-start | bytes 196616 | tf_op jit(solution)/shard_map/ppermute | solution.py:15
  18.0 4.5 %collective-permute-start.2 = (bf16[16,6,1,128]{3,0,2,1:T(8,128)(2,1)S(1)}, bf16[16,6,1,128]{3,0,2,1:T(8,128)(2,1)S(1)}, u32[]{:S(2)}, u32[]{:S(2)}) collective-permute-start(bf16[16,6,1,128]{3,0,2,1:T(8,128)(2,1)S(1)} %get-tuple-element.5), channel_id=1, source_target_pairs={{0,8},{1,9},{2,10},{3,11},{4,12},{5,13},{6,14},{7,15},{16,24},{17,... | collective-permute-start | bytes 73736 | tf_op jit(solution)/shard_map/ppermute | solution.py:14
  21.2 4.6 %collective-permute-start.3 = (bf16[16,6,1,128]{3,0,2,1:T(8,128)(2,1)S(1)}, bf16[16,6,1,128]{3,0,2,1:T(8,128)(2,1)S(1)}, u32[]{:S(2)}, u32[]{:S(2)}) collective-permute-start(bf16[16,6,1,128]{3,0,2,1:T(8,128)(2,1)S(1)} %get-tuple-element.6), channel_id=1, source_target_pairs={{8,0},{9,1},{10,2},{11,3},{12,4},{13,5},{14,6},{15,7},{24,16},{25,... | collective-permute-start | bytes 73736 | tf_op jit(solution)/shard_map/ppermute | solution.py:15
  26.7 47.9 %copy-start.1 = (bf16[3,3,3,16,128]{4,3,2,1,0:T(8,128)(2,1)S(1)}, bf16[3,3,3,16,128]{4,3,2,1,0:T(8,128)(2,1)}, u32[]{:S(2)}) copy-start(bf16[3,3,3,16,128]{4,3,2,1,0:T(8,128)(2,1)} %param.4) | copy-start | bytes 331780
  71.9 2.7 %copy-start = (bf16[128,6,18,128]{3,0,2,1:T(8,128)(2,1)S(1)}, bf16[128,6,18,128]{3,0,2,1:T(8,128)(2,1)}, u32[]{:S(2)}) copy-start(bf16[128,6,18,128]{3,0,2,1:T(8,128)(2,1)} %all-gather.2.cloned.1.call-done) | copy-start | bytes 10616836
  76.3 0.8 copy-start.2
Sparse Core Ops, SparseCore 0:
  26.8 45.0 all-gather.1
where the time goes:
time: 85.4 us; the launch traced here: 85.2 us
  waiting for transfers between devices  51.7 us (61%)
  between operations  13.5 us (16%)
  starting transfers between devices  10.6 us (12%)
  matrix products  4.34 us (5%)
  local copies, waits for them, and re-layouts  3.13 us (4%)
  other arithmetic  1.86 us (2%)
    all_gather x1, waiting for transfers between devices, per_device(): gathered = lax.all_gather(padded, 'col', axis=0, tiled=True)  45.2 us
    ppermute x2, starting transfers between devices, with_halo(): before = lax.ppermute(last, axis, up)  8.02 us
    ppermute x2, waiting for transfers between devices, with_halo(): after = lax.ppermute(first, axis, down)  6.47 us
    dot_general x3, matrix products, convolve(): lax.dot_general(weights[depth_tap], planes, (((3,), (0,)), ((), ())), pre...  4.34 us
    ppermute x2, starting transfers between devices, with_halo(): after = lax.ppermute(first, axis, down)  2.58 us
  transfers between devices with their start and end apart: 5, of which 3 were waited for; matrix products, arithmetic and copies ran while one was open for 1% of the time, Pallas kernels for 0%

commit v1 on v0

--- a/solution.py
+++ b/solution.py
@@ -2,6 +2,19 @@
 import jax.numpy as jnp
 from jax import lax
 from jax.sharding import PartitionSpec as P
+
+
+def ring_gather(x, axis, dim):
+    ways = lax.axis_size(axis)
+    up = [(d, (d + 1) % ways) for d in range(ways)]
+    down = [(d, (d - 1) % ways) for d in range(ways)]
+    earlier, later = ([x], [x])
+    for _ in range(ways // 2):
+        earlier.append(lax.ppermute(earlier[-1], axis, up))
+    for _ in range((ways - 1) // 2):
+        later.append(lax.ppermute(later[-1], axis, down))
+    line = jnp.concatenate([*earlier[::-1], *later[1:]], axis=dim)
+    return jnp.roll(line, (lax.axis_index(axis) - ways // 2) * x.shape[dim], axis=dim)
 
 
 def with_halo(x, sides, width):
@@ -52,7 +65,7 @@
 
 def per_device(features, kernel, channel_bias):
     padded = with_halo(features, (("dev", 1), ("ha", 2)), 1)
-    gathered = lax.all_gather(padded, "col", axis=0, tiled=True)
+    gathered = ring_gather(padded, "col", 0)
     return finish(convolve(gathered, kernel), channel_bias)
 
 

time: 85.4 us -> 68.4 us (0.80)
  the two profiles are of different devices: /device:TPU:1 before, /device:TPU:55 now
where the time goes in v1:
time: 68.4 us; the launch traced here: 68.2 us
  starting transfers between devices  31 us (45%)
  waiting for transfers between devices  28.9 us (42%)
  local copies, waits for them, and re-layouts  4.19 us (6%)
  matrix products  2.54 us (4%)
  other arithmetic  1.24 us (2%)
    ppermute x4, waiting for transfers between devices, ring_gather(): earlier.append(lax.ppermute(earlier[-1], axis, up))  21 us
    ppermute x4, starting transfers between devices, ring_gather(): earlier.append(lax.ppermute(earlier[-1], axis, up))  14.3 us
    ppermute x2, starting transfers between devices, with_halo(): after = lax.ppermute(first, axis, down)  11.5 us
    ppermute x2, starting transfers between devices, with_halo(): before = lax.ppermute(last, axis, up)  5.29 us
    ppermute x2, waiting for transfers between devices, with_halo(): after = lax.ppermute(first, axis, down)  4.81 us
    ppermute x3, waiting for transfers between devices, ring_gather(): later.append(lax.ppermute(later[-1], axis, down))  3.1 us
    dot_general x3, matrix products, convolve(): lax.dot_general(weights[depth_tap], planes, (((3,), (0,)), ((), ())), pre...  2.54 us
    unnamed x21, local copies, waits for them, and re-layouts  2.23 us
  transfers between devices with their start and end apart: 11, of which 7 were waited for; matrix products, arithmetic and copies ran while one was open for 3% of the time, Pallas kernels for 0%

profile of v1, /device:TPU:55, one launch (start us, length us, event | category | flops | bytes accessed | tf_op | source)
XLA Modules:
  0.0 68.2 jit_solution(5121690138902713716)
XLA Ops:
  0.0 0.9 %fusion.27 = (bf16[16,1,16,128]{3,2,1,0:T(8,128)(2,1)S(1)}, bf16[16,1,16,128]{3,2,1,0:T(8,128)(2,1)S(1)}) fusion(bf16[16,4,16,128]{3,2,1,0:T(8,128)(2,1)} %param.3), kind=kLoop, calls=%fused_computation.80 | loop fusion | bytes 262144 | tf_op jit(solution)/shard_map/slice | solution.py:26
  0.9 4.0 %collective-permute-start = (bf16[16,1,16,128]{3,0,2,1:T(8,128)(2,1)S(1)}, bf16[16,1,16,128]{3,0,2,1:T(8,128)(2,1)S(1)}, u32[]{:S(2)}, u32[]{:S(2)}) collective-permute-start(bf16[16,1,16,128]{3,0,2,1:T(8,128)(2,1)S(1)} %copy.37), channel_id=1, source_target_pairs={{0,16},{16,32},{32,48},{48,64},{64,80},{80,96},{96,112},{112,128},... | collective-permute-start | bytes 196616 | tf_op jit(solution)/shard_map/ppermute | solution.py:27
  4.9 10.2 %collective-permute-start.1 = (bf16[16,1,16,128]{3,0,2,1:T(8,128)(2,1)S(1)}, bf16[16,1,16,128]{3,0,2,1:T(8,128)(2,1)S(1)}, u32[]{:S(2)}, u32[]{:S(2)}) collective-permute-start(bf16[16,1,16,128]{3,0,2,1:T(8,128)(2,1)S(1)} %copy.38), channel_id=1, source_target_pairs={{16,0},{32,16},{48,32},{64,48},{80,64},{96,80},{112,96},{128,112},... | collective-permute-start | bytes 196616 | tf_op jit(solution)/shard_map/ppermute | solution.py:28
  15.1 1.1 %constant_dynamic-update-slice_fusion.1 = bf16[16,6,16,128]{3,0,2,1:T(8,128)(2,1)S(1)} fusion(bf16[16,6,16,128]{3,0,2,1:T(8,128)(2,1)S(1)} %constant_dynamic-update-slice_fusion.2, bf16[16,4,16,128]{3,2,1,0:T(8,128)(2,1)} %param.3), kind=kLoop, calls=%fused_computation.52 | loop fusion | bytes 524288
  16.3 1.6 %collective-permute-done.1 = bf16[16,1,16,128]{3,0,2,1:T(8,128)(2,1)S(1)} collective-permute-done((bf16[16,1,16,128]{3,0,2,1:T(8,128)(2,1)S(1)}, bf16[16,1,16,128]{3,0,2,1:T(8,128)(2,1)S(1)}, u32[]{:S(2)}, u32[]{:S(2)}) %collective-permute-start.1) | collective-permute-done | bytes 65568 | tf_op jit(solution)/shard_map/ppermute | solution.py:28
  17.9 1.3 %collective-permute-start.2 = (bf16[16,6,1,128]{3,0,2,1:T(8,128)(2,1)S(1)}, bf16[16,6,1,128]{3,0,2,1:T(8,128)(2,1)S(1)}, u32[]{:S(2)}, u32[]{:S(2)}) collective-permute-start(bf16[16,6,1,128]{3,0,2,1:T(8,128)(2,1)S(1)} %get-tuple-element.5), channel_id=1, source_target_pairs={{0,8},{1,9},{2,10},{3,11},{4,12},{5,13},{6,14},{7,15},{16,24},{17,... | collective-permute-start | bytes 73736 | tf_op jit(solution)/shard_map/ppermute | solution.py:27
  19.2 1.3 %collective-permute-start.3 = (bf16[16,6,1,128]{3,0,2,1:T(8,128)(2,1)S(1)}, bf16[16,6,1,128]{3,0,2,1:T(8,128)(2,1)S(1)}, u32[]{:S(2)}, u32[]{:S(2)}) collective-permute-start(bf16[16,6,1,128]{3,0,2,1:T(8,128)(2,1)S(1)} %get-tuple-element.6), channel_id=1, source_target_pairs={{8,0},{9,1},{10,2},{11,3},{12,4},{13,5},{14,6},{15,7},{24,16},{25,... | collective-permute-start | bytes 73736 | tf_op jit(solution)/shard_map/ppermute | solution.py:28
  20.5 3.3 %collective-permute-done.3 = bf16[16,6,1,128]{3,0,2,1:T(8,128)(2,1)S(1)} collective-permute-done((bf16[16,6,1,128]{3,0,2,1:T(8,128)(2,1)S(1)}, bf16[16,6,1,128]{3,0,2,1:T(8,128)(2,1)S(1)}, u32[]{:S(2)}, u32[]{:S(2)}) %collective-permute-start.3) | collective-permute-done | bytes 24608 | tf_op jit(solution)/shard_map/ppermute | solution.py:28
  23.8 3.2 %collective-permute-start.4 = (bf16[16,6,18,128]{3,0,2,1:T(8,128)(2,1)S(1)}, bf16[16,6,18,128]{3,0,2,1:T(8,128)(2,1)S(1)}, u32[]{:S(2)}, u32[]{:S(2)}) collective-permute-start(bf16[16,6,18,128]{3,0,2,1:T(8,128)(2,1)S(1)} %pad_maximum_fusion), channel_id=1, source_target_pairs={{0,1},{1,2},{2,3},{3,4},{4,5},{5,6},{6,7},{7,0},{8,9},{9,10},{10,1... | collective-permute-start | bytes 1327112 | tf_op jit(solution)/shard_map/ppermute | solution.py:13
  27.0 5.2 %collective-permute-done.4 = bf16[16,6,18,128]{3,0,2,1:T(8,128)(2,1)S(1)} collective-permute-done((bf16[16,6,18,128]{3,0,2,1:T(8,128)(2,1)S(1)}, bf16[16,6,18,128]{3,0,2,1:T(8,128)(2,1)S(1)}, u32[]{:S(2)}, u32[]{:S(2)}) %collective-permute-start.4) | collective-permute-done | bytes 442400 | tf_op jit(solution)/shard_map/ppermute | solution.py:13
  32.2 3.7 %collective-permute-start.5 = (bf16[16,6,18,128]{3,0,2,1:T(8,128)(2,1)S(1)}, bf16[16,6,18,128]{3,0,2,1:T(8,128)(2,1)S(1)}, u32[]{:S(2)}, u32[]{:S(2)}) collective-permute-start(bf16[16,6,18,128]{3,0,2,1:T(8,128)(2,1)S(1)} %collective-permute-done.4), channel_id=1, source_target_pairs={{0,1},{1,2},{2,3},{3,4},{4,5},{5,6},{6,7},{7,0},{8,9},{9,10},{10,1... | collective-permute-start | bytes 1327112 | tf_op jit(solution)/shard_map/ppermute | solution.py:13
  35.9 5.2 %collective-permute-done.5 = bf16[16,6,18,128]{3,0,2,1:T(8,128)(2,1)S(1)} collective-permute-done((bf16[16,6,18,128]{3,0,2,1:T(8,128)(2,1)S(1)}, bf16[16,6,18,128]{3,0,2,1:T(8,128)(2,1)S(1)}, u32[]{:S(2)}, u32[]{:S(2)}) %collective-permute-start.5) | collective-permute-done | bytes 442400 | tf_op jit(solution)/shard_map/ppermute | solution.py:13
  41.2 3.7 %collective-permute-start.6 = (bf16[16,6,18,128]{3,0,2,1:T(8,128)(2,1)S(1)}, bf16[16,6,18,128]{3,0,2,1:T(8,128)(2,1)S(1)}, u32[]{:S(2)}, u32[]{:S(2)}) collective-permute-start(bf16[16,6,18,128]{3,0,2,1:T(8,128)(2,1)S(1)} %collective-permute-done.5), channel_id=1, source_target_pairs={{0,1},{1,2},{2,3},{3,4},{4,5},{5,6},{6,7},{7,0},{8,9},{9,10},{10,1... | collective-permute-start | bytes 1327112 | tf_op jit(solution)/shard_map/ppermute | solution.py:13
  44.9 5.2 %collective-permute-done.6 = bf16[16,6,18,128]{3,0,2,1:T(8,128)(2,1)S(1)} collective-permute-done((bf16[16,6,18,128]{3,0,2,1:T(8,128)(2,1)S(1)}, bf16[16,6,18,128]{3,0,2,1:T(8,128)(2,1)S(1)}, u32[]{:S(2)}, u32[]{:S(2)}) %collective-permute-start.6) | collective-permute-done | bytes 442400 | tf_op jit(solution)/shard_map/ppermute | solution.py:13
  50.1 3.7 %collective-permute-start.7 = (bf16[16,6,18,128]{3,0,2,1:T(8,128)(2,1)S(1)}, bf16[16,6,18,128]{3,0,2,1:T(8,128)(2,1)S(1)}, u32[]{:S(2)}, u32[]{:S(2)}) collective-permute-start(bf16[16,6,18,128]{3,0,2,1:T(8,128)(2,1)S(1)} %collective-permute-done.6), channel_id=1, source_target_pairs={{0,1},{1,2},{2,3},{3,4},{4,5},{5,6},{6,7},{7,0},{8,9},{9,10},{10,1... | collective-permute-start | bytes 1327112 | tf_op jit(solution)/shard_map/ppermute | solution.py:13
  53.8 5.2 %collective-permute-done.7 = bf16[16,6,18,128]{3,0,2,1:T(8,128)(2,1)S(1)} collective-permute-done((bf16[16,6,18,128]{3,0,2,1:T(8,128)(2,1)S(1)}, bf16[16,6,18,128]{3,0,2,1:T(8,128)(2,1)S(1)}, u32[]{:S(2)}, u32[]{:S(2)}) %collective-permute-start.7) | collective-permute-done | bytes 442400 | tf_op jit(solution)/shard_map/ppermute | solution.py:13
  59.1 0.1 constant_dynamic-update-slice_fusion.17
  59.3 0.1 constant_dynamic-update-slice_fusion.15
  59.4 0.1 constant_dynamic-update-slice_fusion.14
  59.5 0.1 constant_dynamic-update-slice_fusion.13
  59.6 0.1 constant_dynamic-update-slice_fusion.12
  59.7 3.1 %collective-permute-done.10 = bf16[16,6,18,128]{3,0,2,1:T(8,128)(2,1)S(1)} collective-permute-done((bf16[16,6,18,128]{3,0,2,1:T(8,128)(2,1)S(1)}, bf16[16,6,18,128]{3,0,2,1:T(8,128)(2,1)S(1)}, u32[]{:S(2)}, u32[]{:S(2)}) %collective-permute-start.10) | collective-permute-done | bytes 442400 | tf_op jit(solution)/shard_map/ppermute | solution.py:15
  62.8 0.1 constant_dynamic-update-slice_fusion.10
  63.2 0.1 constant_dynamic-update-slice_fusion.6
  63.6 0.8 %convolution_bitcast_fusion.2 = f32[3,3,16,4,18,128]{5,2,1,0,4,3:T(8,128)S(1)} fusion(bf16[256,6,18,128]{3,0,2,1:T(8,128)(2,1)S(1)} %constant_dynamic-update-slice_fusion.3, s32[]{:T(128)S(6)} %select_n.18, bf16[3,3,3,16,128]{4,3,2,1,0:T(8,128)(2,1)S(1)} %copy-done), kind=kOutput, calls=%fused_computation.2 | convolution fusion | flops 339738624 | bytes 7704580 | tf_op jit(solution)/shard_map/dot_general | solution.py:46
  64.4 0.8 %convolution_bitcast_fusion.1 = f32[3,3,16,4,18,128]{5,2,4,3,1,0:T(8,128)S(1)} fusion(bf16[256,6,18,128]{3,0,2,1:T(8,128)(2,1)S(1)} %constant_dynamic-update-slice_fusion.3, s32[]{:T(128)S(6)} %select_n.18, s32[]{:T(128)S(6)} %add.164, bf16[3,3,3,16,128]{4,3,2,1,0:T(8,128)(2,1)S(1)} %copy-done), kind=kOutput, calls=%fused_computation.1 | convolution fusion | flops 339738624 | bytes 7704584 | tf_op jit(solution)/shard_map/dot_general | solution.py:46
  65.3 0.8 %convolution_bitcast_fusion = f32[3,3,16,4,18,128]{5,2,4,3,1,0:T(8,128)S(1)} fusion(bf16[256,6,18,128]{3,0,2,1:T(8,128)(2,1)S(1)} %constant_dynamic-update-slice_fusion.3, s32[]{:T(128)S(6)} %select_n.18, s32[]{:T(128)S(6)} %add.165, bf16[3,3,3,16,128]{4,3,2,1,0:T(8,128)(2,1)S(1)} %copy-done), kind=kOutput, calls=%fused_computation | convolution fusion | flops 339738624 | bytes 7704584 | tf_op jit(solution)/shard_map/dot_general | solution.py:46
  66.2 0.3 fusion.2
  66.5 0.3 fusion.8
  66.8 0.2 slice.188
  67.0 0.4 fusion
  67.4 0.8 %copy.21 = bf16[16,4,16,128]{3,2,1,0:T(8,128)(2,1)} copy(bf16[16,4,16,128]{3,0,2,1:T(8,128)(2,1)S(1)} %fusion) | data formatting | bytes 524288 | tf_op jit(solution)/shard_map/convert_element_type | solution.py:63
  (26 shorter events, 0.9 us)
Async XLA Ops:
  0.9 14.2 %collective-permute-start = (bf16[16,1,16,128]{3,0,2,1:T(8,128)(2,1)S(1)}, bf16[16,1,16,128]{3,0,2,1:T(8,128)(2,1)S(1)}, u32[]{:S(2)}, u32[]{:S(2)}) collective-permute-start(bf16[16,1,16,128]{3,0,2,1:T(8,128)(2,1)S(1)} %copy.37), channel_id=1, source_target_pairs={{0,16},{16,32},{32,48},{48,64},{64,80},{80,96},{96,112},{112,128},... | collective-permute-start | bytes 196616 | tf_op jit(solution)/shard_map/ppermute | solution.py:27
  4.9 12.9 %collective-permute-start.1 = (bf16[16,1,16,128]{3,0,2,1:T(8,128)(2,1)S(1)}, bf16[16,1,16,128]{3,0,2,1:T(8,128)(2,1)S(1)}, u32[]{:S(2)}, u32[]{:S(2)}) collective-permute-start(bf16[16,1,16,128]{3,0,2,1:T(8,128)(2,1)S(1)} %copy.38), channel_id=1, source_target_pairs={{16,0},{32,16},{48,32},{64,48},{80,64},{96,80},{112,96},{128,112},... | collective-permute-start | bytes 196616 | tf_op jit(solution)/shard_map/ppermute | solution.py:28
  17.9 2.6 %collective-permute-start.2 = (bf16[16,6,1,128]{3,0,2,1:T(8,128)(2,1)S(1)}, bf16[16,6,1,128]{3,0,2,1:T(8,128)(2,1)S(1)}, u32[]{:S(2)}, u32[]{:S(2)}) collective-permute-start(bf16[16,6,1,128]{3,0,2,1:T(8,128)(2,1)S(1)} %get-tuple-element.5), channel_id=1, source_target_pairs={{0,8},{1,9},{2,10},{3,11},{4,12},{5,13},{6,14},{7,15},{16,24},{17,... | collective-permute-start | bytes 73736 | tf_op jit(solution)/shard_map/ppermute | solution.py:27
  19.2 4.6 %collective-permute-start.3 = (bf16[16,6,1,128]{3,0,2,1:T(8,128)(2,1)S(1)}, bf16[16,6,1,128]{3,0,2,1:T(8,128)(2,1)S(1)}, u32[]{:S(2)}, u32[]{:S(2)}) collective-permute-start(bf16[16,6,1,128]{3,0,2,1:T(8,128)(2,1)S(1)} %get-tuple-element.6), channel_id=1, source_target_pairs={{8,0},{9,1},{10,2},{11,3},{12,4},{13,5},{14,6},{15,7},{24,16},{25,... | collective-permute-start | bytes 73736 | tf_op jit(solution)/shard_map/ppermute | solution.py:28
  23.8 8.4 %collective-permute-start.4 = (bf16[16,6,18,128]{3,0,2,1:T(8,128)(2,1)S(1)}, bf16[16,6,18,128]{3,0,2,1:T(8,128)(2,1)S(1)}, u32[]{:S(2)}, u32[]{:S(2)}) collective-permute-start(bf16[16,6,18,128]{3,0,2,1:T(8,128)(2,1)S(1)} %pad_maximum_fusion), channel_id=1, source_target_pairs={{0,1},{1,2},{2,3},{3,4},{4,5},{5,6},{6,7},{7,0},{8,9},{9,10},{10,1... | collective-permute-start | bytes 1327112 | tf_op jit(solution)/shard_map/ppermute | solution.py:13
  32.2 8.9 %collective-permute-start.5 = (bf16[16,6,18,128]{3,0,2,1:T(8,128)(2,1)S(1)}, bf16[16,6,18,128]{3,0,2,1:T(8,128)(2,1)S(1)}, u32[]{:S(2)}, u32[]{:S(2)}) collective-permute-start(bf16[16,6,18,128]{3,0,2,1:T(8,128)(2,1)S(1)} %collective-permute-done.4), channel_id=1, source_target_pairs={{0,1},{1,2},{2,3},{3,4},{4,5},{5,6},{6,7},{7,0},{8,9},{9,10},{10,1... | collective-permute-start | bytes 1327112 | tf_op jit(solution)/shard_map/ppermute | solution.py:13
  35.9 8.9 %collective-permute-start.8 = (bf16[16,6,18,128]{3,0,2,1:T(8,128)(2,1)S(1)}, bf16[16,6,18,128]{3,0,2,1:T(8,128)(2,1)S(1)}, u32[]{:S(2)}, u32[]{:S(2)}) collective-permute-start(bf16[16,6,18,128]{3,0,2,1:T(8,128)(2,1)S(1)} %pad_maximum_fusion), channel_id=1, source_target_pairs={{0,7},{1,0},{2,1},{3,2},{4,3},{5,4},{6,5},{7,6},{8,15},{9,8},{10,9... | collective-permute-start | bytes 1327112 | tf_op jit(solution)/shard_map/ppermute | solution.py:15
  41.2 8.9 %collective-permute-start.6 = (bf16[16,6,18,128]{3,0,2,1:T(8,128)(2,1)S(1)}, bf16[16,6,18,128]{3,0,2,1:T(8,128)(2,1)S(1)}, u32[]{:S(2)}, u32[]{:S(2)}) collective-permute-start(bf16[16,6,18,128]{3,0,2,1:T(8,128)(2,1)S(1)} %collective-permute-done.5), channel_id=1, source_target_pairs={{0,1},{1,2},{2,3},{3,4},{4,5},{5,6},{6,7},{7,0},{8,9},{9,10},{10,1... | collective-permute-start | bytes 1327112 | tf_op jit(solution)/shard_map/ppermute | solution.py:13
  44.9 8.9 %collective-permute-start.9 = (bf16[16,6,18,128]{3,0,2,1:T(8,128)(2,1)S(1)}, bf16[16,6,18,128]{3,0,2,1:T(8,128)(2,1)S(1)}, u32[]{:S(2)}, u32[]{:S(2)}) collective-permute-start(bf16[16,6,18,128]{3,0,2,1:T(8,128)(2,1)S(1)} %collective-permute-done.8), channel_id=1, source_target_pairs={{0,7},{1,0},{2,1},{3,2},{4,3},{5,4},{6,5},{7,6},{8,15},{9,8},{10,9... | collective-permute-start | bytes 1327112 | tf_op jit(solution)/shard_map/ppermute | solution.py:15
  50.1 8.9 %collective-permute-start.7 = (bf16[16,6,18,128]{3,0,2,1:T(8,128)(2,1)S(1)}, bf16[16,6,18,128]{3,0,2,1:T(8,128)(2,1)S(1)}, u32[]{:S(2)}, u32[]{:S(2)}) collective-permute-start(bf16[16,6,18,128]{3,0,2,1:T(8,128)(2,1)S(1)} %collective-permute-done.6), channel_id=1, source_target_pairs={{0,1},{1,2},{2,3},{3,4},{4,5},{5,6},{6,7},{7,0},{8,9},{9,10},{10,1... | collective-permute-start | bytes 1327112 | tf_op jit(solution)/shard_map/ppermute | solution.py:13
  53.8 9.8 %copy-start = (bf16[3,3,3,16,128]{4,3,2,1,0:T(8,128)(2,1)S(1)}, bf16[3,3,3,16,128]{4,3,2,1,0:T(8,128)(2,1)}, u32[]{:S(2)}) copy-start(bf16[3,3,3,16,128]{4,3,2,1,0:T(8,128)(2,1)} %param.4) | copy-start | bytes 331780
  53.8 8.9 %collective-permute-start.10 = (bf16[16,6,18,128]{3,0,2,1:T(8,128)(2,1)S(1)}, bf16[16,6,18,128]{3,0,2,1:T(8,128)(2,1)S(1)}, u32[]{:S(2)}, u32[]{:S(2)}) collective-permute-start(bf16[16,6,18,128]{3,0,2,1:T(8,128)(2,1)S(1)} %collective-permute-done.9), channel_id=1, source_target_pairs={{0,7},{1,0},{2,1},{3,2},{4,3},{5,4},{6,5},{7,6},{8,15},{9,8},{10,9... | collective-permute-start | bytes 1327112 | tf_op jit(solution)/shard_map/ppermute | solution.py:15
  66.1 0.8 %copy-start.1 = (f32[16]{0:T(128)S(1)}, f32[16]{0:T(128)}, u32[]{:S(2)}) copy-start(f32[16]{0:T(128)} %param.5) | copy-start | bytes 196
